TPU v7x, 256 devices: a whole 4x4x8 slice. The times are simulated.
256 devices in a mesh: group: 8 (over y, core), dev: 32 (over x, z).
Axes of the slice: x: 4, y: 4, z: 8, core: 2. Of those that a mesh axis runs over, the one named last changes fastest.
Arguments:
- tiles: float32 [524288, 3, 128], P(('group', 'dev')), may hold values from -6 to 6
- levels: int32 [524288], P(('group', 'dev')), may hold values from 0 to 2
- new_owner: int32 [524288], P(('group', 'dev')), may hold values from 0 to 31, as said below
- new_slot: int32 [524288], P(('group', 'dev')), may hold values from 0 to 2047
- flags: int32 [524288], P(('group', 'dev')), may hold values 0 or 1
- halo_source: int32 [256, 2, 64], P(('group', 'dev')), may hold values from 0 to 2047
- halo_target: int32 [256, 2, 64], P(('group', 'dev')), may hold values from 0 to 2047
- halo_count: int32 [256, 2], P(('group', 'dev')), may hold values from 1 to 64, as said below
- stiffness: float32 [3, 384, 384], replicated, may hold values from -0.3125 to 0.3125
- nitsche: float32 [384, 384], replicated, may hold values from -0.3125 to 0.3125
- coupling: float32 [384, 384], replicated, may hold values from -0.3125 to 0.3125
Outputs:
- first: float32 [524288, 3, 128], P(('group', 'dev'))
- second: float32 [524288, 3, 128], P(('group', 'dev'))
Inputs may be any that keep to these rules, and one draw needn't show every extreme that they name: Within each group, new_owner and new_slot place the group's tiles one to one on its devices' 2048 positions; each device sends at most 80 tiles to one device of its group, and some send exactly 80. `halo_count`: some device's list in each direction holds 64 entries.
All inputs are finite; a program needn't handle non-finite values. No bound on the sum of `flags` on one device may be relied on, other than what follows from the above.
Results may differ from a plain program's by a relative error of at most 0.0001.
Values sent between devices are 32-bit elements; how exact they have to be, the bound alone decides.
A program may use at most 128 MiB of HBM per device.

v0:
```python
import functools

import jax
import jax.numpy as jnp
from jax import lax
from jax.experimental import pallas as pl
from jax.experimental.pallas import tpu as pltpu
from jax.sharding import PartitionSpec as P

MESH = pl.DeviceIdType.MESH
LANES = 128
PAD = 8
ROWS = 256
NZ = 8
VMEM_LIMIT = 56 << 20
F32, BF16, I32 = jnp.float32, jnp.bfloat16, jnp.int32


def vmem():
    return pl.BlockSpec(memory_space=pltpu.VMEM)


def smem():
    return pl.BlockSpec(memory_space=pltpu.SMEM)


def hbm():
    return pl.BlockSpec(memory_space=pl.ANY)


def iota(shape, axis):
    return lax.broadcasted_iota(I32, shape, axis)


def nt_dot(a, b):
    return lax.dot_general(a, b, (((1,), (1,)), ((), ())), preferred_element_type=F32)


def dot(a, b):
    return jnp.dot(a, b, preferred_element_type=F32)


def halves(value):
    high = value.astype(BF16)
    return high, (value - high.astype(F32)).astype(BF16)


def plan_kernel(ndev, owner_ref, slot_ref, level_ref, source_ref, meta_ref):
    blocks = owner_ref.shape[0]
    before = (iota((LANES, LANES), 0) < iota((LANES, LANES), 1)).astype(F32).astype(BF16)
    running = jnp.zeros((ndev, 1), F32)
    source = jnp.zeros((2 * ndev, LANES), F32)
    meta = jnp.zeros((8 * ndev, LANES), F32)
    kind = iota((8 * ndev, LANES), 0) % 8
    dest8 = iota((8 * ndev, LANES), 0) // 8
    dest = iota((ndev, LANES), 0)
    for b in range(blocks):
        owner = owner_ref[b : b + 1, :]
        mine = (owner == dest).astype(F32)
        earlier = dot(mine.astype(BF16), before) + running
        running = running + jnp.sum(mine, axis=1, keepdims=True)
        rank = jnp.sum(mine * earlier, axis=0, keepdims=True).astype(I32)
        place = (rank == iota((LANES, LANES), 0)).astype(F32).astype(BF16)
        lane = iota((1, LANES), 1).astype(F32)
        source = source + nt_dot(
            jnp.concatenate([mine * float(b), mine * lane], axis=0).astype(BF16), place
        )
        slot = slot_ref[b : b + 1, :]
        high = (slot // LANES + 1).astype(F32)
        low = (slot % LANES).astype(F32)
        level = level_ref[b : b + 1, :].astype(F32)
        entry = jnp.where(kind == 0, high, jnp.where(kind == 1, low, jnp.where(kind == 2, level, 0.0)))
        entry = jnp.where(owner == dest8, entry, 0.0)
        meta = meta + nt_dot(entry.astype(BF16), place)
    source_ref[...] = (source[:ndev] * float(LANES) + source[ndev:]).astype(I32)
    meta_ref[...] = meta


def exchange_kernel(
    ndev,
    capacity,
    source_ref,
    tiles_ref,
    meta_ref,
    flags_ref,
    stiffness_ref,
    nitsche_ref,
    coupling_ref,
    recv_ref,
    inverse_ref,
    masks_ref,
    weights_ref,
    send_ref,
    meta_recv_ref,
    send_sem,
    recv_sem,
    meta_send_sem,
    meta_recv_sem,
    own_sem,
):
    me = lax.axis_index("dev")
    x, z = me // NZ, me % NZ
    nx = ndev // NZ
    chunk = 3 * capacity

    def offset(step):
        return (11 * step) % ndev

    def peer(off):
        return ((x + off // NZ) % nx) * NZ + (z + off % NZ) % NZ

    def rows_of(off):
        return pl.ds(pl.multiple_of(off * chunk, 8), chunk)

    def meta_copy(step):
        off = offset(step)
        to = peer(off)
        return pltpu.make_async_remote_copy(
            src_ref=meta_ref.at[pl.ds(pl.multiple_of(to * 8, 8), 8)],
            dst_ref=meta_recv_ref.at[pl.ds(pl.multiple_of(off * 8, 8), 8)],
            send_sem=meta_send_sem.at[off],
            recv_sem=meta_recv_sem.at[off],
            device_id={"dev": to},
            device_id_type=MESH,
        )

    def data_copy(step):
        off = offset(step)
        return pltpu.make_async_remote_copy(
            src_ref=send_ref.at[rows_of(off)],
            dst_ref=recv_ref.at[rows_of(off)],
            send_sem=send_sem.at[off],
            recv_sem=recv_sem.at[off],
            device_id={"dev": peer(off)},
            device_id_type=MESH,
        )

    def pack(off):
        to = peer(off)
        base = pl.multiple_of(off * chunk, 8)
        for k in range(capacity):
            row = source_ref[to, k]
            for p in range(3):
                send_ref[pl.ds(base + (p * capacity + k), 1), :] = tiles_ref[p, pl.ds(row, 1), :]

    barrier = pltpu.get_barrier_semaphore()

    @pl.loop(1, ndev)
    def _(step):
        pl.semaphore_signal(
            barrier, inc=1, device_id={"dev": peer(offset(step))}, device_id_type=MESH
        )

    pl.semaphore_wait(barrier, ndev - 1)

    @pl.loop(1, ndev)
    def _(step):
        meta_copy(step).start()

    @pl.loop(1, ndev)
    def _(step):
        pack(offset(step))

        @pl.when(step > 1)
        def _():
            data_copy(step - 1).start()

    pack(0)
    data_copy(ndev - 1).start()
    own_rows = pltpu.make_async_copy(send_ref.at[rows_of(0)], recv_ref.at[rows_of(0)], own_sem.at[0])
    own_meta = pltpu.make_async_copy(
        meta_ref.at[pl.ds(pl.multiple_of(me * 8, 8), 8)], meta_recv_ref.at[pl.ds(0, 8)], own_sem.at[1]
    )
    own_meta.start()

    for group in range(5):
        weight = stiffness_ref[group] if group < 3 else (nitsche_ref, coupling_ref)[group - 3][...]
        high, low = halves(weight)
        weights_ref[pl.ds(group * 384, 384), 0:384] = high
        weights_ref[pl.ds(group * 384, 384), 384:768] = low
    own_rows.start()

    own_meta.wait()

    @pl.loop(1, ndev)
    def _(step):
        meta_copy(step).wait()

    blocks = flags_ref.shape[0]
    kind = iota((3 * blocks, LANES), 0) // blocks
    high_of = iota((3 * blocks, LANES), 0) % blocks + 1
    rank = iota((1, LANES), 1)

    def place(off, total):
        base = pl.multiple_of(off * 8, 8)
        meta = meta_recv_ref[pl.ds(base, 8), :]
        high, low, level = meta[0:1].astype(I32), meta[1:2].astype(I32), meta[2:3]
        value = jnp.where(
            kind == 0,
            jnp.full((1, LANES), off, I32).astype(F32),
            jnp.where(kind == 1, rank.astype(F32), level),
        )
        value = jnp.where(high == high_of, value, 0.0)
        column = (low == iota((LANES, LANES), 0)).astype(F32)
        return total + nt_dot(value.astype(BF16), column.astype(BF16))

    total = lax.fori_loop(0, ndev, place, jnp.zeros((3 * blocks, LANES), F32))
    inverse_ref[...] = (total[:blocks] * float(chunk) + total[blocks : 2 * blocks]).astype(I32)
    level = total[2 * blocks :]
    masks_ref[...] = jnp.concatenate(
        [(level == float(index)).astype(F32) for index in range(3)] + [flags_ref[...].astype(F32)],
        axis=0,
    )

    own_rows.wait()

    @pl.loop(1, ndev)
    def _(step):
        data_copy(step).wait()


def gather_kernel(capacity, inverse_ref, recv_ref, field_ref):
    blocks = inverse_ref.shape[0]
    count = blocks * LANES
    for p in range(3):
        field_ref[p, 0:PAD, :] = jnp.zeros((PAD, LANES), F32)
        field_ref[p, PAD + count : 2 * PAD + count, :] = jnp.zeros((PAD, LANES), F32)

    @pl.loop(0, blocks)
    def _(block):
        base = pl.multiple_of(block * LANES, 8)
        for k in range(LANES):
            row = inverse_ref[block, k]
            for p in range(3):
                field_ref[p, pl.ds(base + (PAD + k), 1), :] = recv_ref[pl.ds(row + p * capacity, 1), :]


def operator_block(field_ref, masks_ref, weights_ref, block):
    base = pl.multiple_of(block * ROWS, ROWS)
    columns = masks_ref[pl.ds(pl.multiple_of(block * ROWS, ROWS), ROWS), :]
    masks = [columns[:, l : l + 1].astype(BF16) for l in range(4)]
    high, low, beside_high, beside_low = [], [], [], []
    for p in range(3):
        wide = field_ref[p, pl.ds(base, ROWS + 2 * PAD), :]
        h, l = halves(wide[PAD : PAD + ROWS])
        high.append(h)
        low.append(l)
        h, l = halves(wide[PAD - 1 : PAD - 1 + ROWS] + wide[PAD + 1 : PAD + 1 + ROWS])
        beside_high.append(h)
        beside_low.append(l)
    left = jnp.concatenate([h * m for m in masks for h in high] + beside_high, axis=1)
    result = dot(left, weights_ref[...])
    left = jnp.concatenate([l * m for m in masks for l in low] + beside_low, axis=1)
    return result[:, :384] + result[:, 384:] + dot(left, weights_ref[:, 0:384])


def halo_images(arrived_ref, weights_ref, images_ref, has_prev, has_next, halo):
    rows = []
    for side, alive in ((0, has_prev), (1, has_next)):
        row = jnp.concatenate(
            [arrived_ref[side, pl.ds(p * halo, halo), :] for p in range(3)], axis=1
        )
        rows.append(jnp.where(alive, row, 0.0))
    high, low = halves(jnp.concatenate(rows, axis=0))
    result = dot(high, weights_ref[1536:1920, :])
    images = result[:, :384] + result[:, 384:] + dot(low, weights_ref[1536:1920, 0:384])
    high, low = halves(images)
    images_ref[0 : 2 * halo, :] = high
    images_ref[2 * halo : 4 * halo, :] = low


def halo_block(target_ref, images_ref, block):
    halo2 = target_ref.shape[1]
    rows = iota((ROWS, halo2), 0) + block * ROWS
    chosen = (rows == target_ref[...]).astype(F32).astype(BF16)
    return dot(jnp.concatenate([chosen, chosen], axis=1), images_ref[...])


def neighbours(groups, ndev):
    group, dev = lax.axis_index("group"), lax.axis_index("dev")
    me = group * ndev + dev
    total = groups * ndev
    after, prior = (me + 1) % total, (me + total - 1) % total
    return me, (prior // ndev, prior % ndev), (after // ndev, after % ndev)


def first_kernel(
    groups,
    ndev,
    source_ref,
    count_ref,
    field_ref,
    masks_ref,
    weights_ref,
    target_ref,
    first_ref,
    second_halo_ref,
    send_ref,
    arrived_ref,
    arrived2_ref,
    images_ref,
    send_sem,
    recv_sem,
):
    halo = source_ref.shape[1]
    blocks = (field_ref.shape[1] - 2 * PAD) // ROWS
    me, prior, after = neighbours(groups, ndev)
    has_prev, has_next = me > 0, me < groups * ndev - 1

    barrier = pltpu.get_barrier_semaphore()
    for other in (prior, after):
        pl.semaphore_signal(barrier, inc=1, device_id=other, device_id_type=MESH)
    pl.semaphore_wait(barrier, 2)

    def copies(turn, into):
        return [
            pltpu.make_async_remote_copy(
                src_ref=send_ref.at[turn, side],
                dst_ref=into.at[1 - side],
                send_sem=send_sem.at[turn, side],
                recv_sem=recv_sem.at[turn, side],
                device_id=(prior, after)[side],
                device_id_type=MESH,
            )
            for side in range(2)
        ]

    def pack(turn, rows_ref):
        for side in range(2):
            for k in range(halo):
                row = source_ref[side, k] + PAD
                for p in range(3):
                    send_ref[turn, side, pl.ds(p * halo + k, 1), :] = rows_ref[p, pl.ds(row, 1), :]
            live = iota((halo, LANES), 0) < count_ref[0, side]
            for p in range(3):
                part = pl.ds(p * halo, halo)
                send_ref[turn, side, part, :] = jnp.where(live, send_ref[turn, side, part, :], 0.0)

    def local(block):
        result = operator_block(field_ref, masks_ref, weights_ref, block)
        rows = pl.ds(pl.multiple_of(block * ROWS, ROWS) + PAD, ROWS)
        for p in range(3):
            first_ref[p, rows, :] = result[:, p * LANES : (p + 1) * LANES]

    pack(0, field_ref)
    for p in range(3):
        first_ref[p, 0:PAD, :] = jnp.zeros((PAD, LANES), F32)
        first_ref[p, PAD + blocks * ROWS : 2 * PAD + blocks * ROWS, :] = jnp.zeros((PAD, LANES), F32)
    local(0)
    sent = copies(0, arrived_ref)
    for copy in sent:
        copy.start()

    @pl.loop(1, blocks)
    def _(block):
        local(block)

    for copy in sent:
        copy.wait()
    halo_images(arrived_ref, weights_ref, images_ref, has_prev, has_next, halo)

    @pl.loop(0, blocks)
    def _(block):
        added = halo_block(target_ref, images_ref, block)
        rows = pl.ds(pl.multiple_of(block * ROWS, ROWS) + PAD, ROWS)
        for p in range(3):
            first_ref[p, rows, :] = first_ref[p, rows, :] + added[:, p * LANES : (p + 1) * LANES]

    pack(1, first_ref)
    sent = copies(1, arrived2_ref)
    for copy in sent:
        copy.start()
    for copy in sent:
        copy.wait()
    second_halo_ref[...] = arrived2_ref[...]


def second_kernel(
    groups,
    ndev,
    field_ref,
    masks_ref,
    weights_ref,
    target_ref,
    arrived_ref,
    first_ref,
    second_ref,
    images_ref,
):
    halo = arrived_ref.shape[1] // 3
    block = pl.program_id(0)

    @pl.when(block == 0)
    def _():
        me, _, _ = neighbours(groups, ndev)
        halo_images(arrived_ref, weights_ref, images_ref, me > 0, me < groups * ndev - 1, halo)

    result = operator_block(field_ref, masks_ref, weights_ref, block)
    result = result + halo_block(target_ref, images_ref, block)
    rows = pl.ds(pl.multiple_of(block * ROWS, ROWS) + PAD, ROWS)
    for p in range(3):
        first_ref[p] = field_ref[p, rows, :]
        second_ref[p] = result[:, p * LANES : (p + 1) * LANES]


def local(
    groups,
    ndev,
    tiles,
    levels,
    new_owner,
    new_slot,
    flags,
    halo_source,
    halo_target,
    halo_count,
    stiffness,
    nitsche,
    coupling,
):
    count = tiles.shape[0]
    halo = halo_source.shape[2]
    blocks = count // LANES
    capacity = count // ndev + count // (4 * ndev)
    planes = jnp.transpose(tiles, (1, 0, 2))
    by_lane = (blocks, LANES)
    shape = jax.ShapeDtypeStruct

    source, meta = pl.pallas_call(
        functools.partial(plan_kernel, ndev),
        out_shape=(shape((ndev, LANES), I32), shape((8 * ndev, LANES), F32)),
        in_specs=[vmem()] * 3,
        out_specs=(vmem(), vmem()),
        name="plan",
    )(new_owner.reshape(by_lane), new_slot.reshape(by_lane), levels.reshape(by_lane))

    arrivals = ndev * 3 * capacity
    recv, inverse, masks, weights = pl.pallas_call(
        functools.partial(exchange_kernel, ndev, capacity),
        out_shape=(
            shape((arrivals, LANES), F32),
            shape(by_lane, I32),
            shape((4 * blocks, LANES), F32),
            shape((1920, 768), BF16),
        ),
        in_specs=[smem()] + [vmem()] * 6,
        out_specs=(hbm(), vmem(), vmem(), vmem()),
        scratch_shapes=[
            pltpu.VMEM((arrivals, LANES), F32),
            pltpu.VMEM((8 * ndev, LANES), F32),
            pltpu.SemaphoreType.DMA((ndev,)),
            pltpu.SemaphoreType.DMA((ndev,)),
            pltpu.SemaphoreType.DMA((ndev,)),
            pltpu.SemaphoreType.DMA((ndev,)),
            pltpu.SemaphoreType.DMA((2,)),
        ],
        compiler_params=pltpu.CompilerParams(
            collective_id=0, has_side_effects=True, vmem_limit_bytes=VMEM_LIMIT
        ),
        name="exchange",
    )(source, planes, meta, flags.reshape(by_lane), stiffness, nitsche, coupling)

    field = pl.pallas_call(
        functools.partial(gather_kernel, capacity),
        out_shape=shape((3, count + 2 * PAD, LANES), F32),
        in_specs=[smem(), vmem()],
        out_specs=vmem(),
        compiler_params=pltpu.CompilerParams(vmem_limit_bytes=VMEM_LIMIT),
        name="gather",
    )(inverse, recv)

    masks = masks.reshape(4, count).T
    targets = halo_target.reshape(1, 2 * halo)
    first, second_halo = pl.pallas_call(
        functools.partial(first_kernel, groups, ndev),
        out_shape=(shape(field.shape, F32), shape((2, 3 * halo, LANES), F32)),
        in_specs=[smem(), smem()] + [vmem()] * 4,
        out_specs=(vmem(), vmem()),
        scratch_shapes=[
            pltpu.VMEM((2, 2, 3 * halo, LANES), F32),
            pltpu.VMEM((2, 3 * halo, LANES), F32),
            pltpu.VMEM((2, 3 * halo, LANES), F32),
            pltpu.VMEM((4 * halo, 384), BF16),
            pltpu.SemaphoreType.DMA((2, 2)),
            pltpu.SemaphoreType.DMA((2, 2)),
        ],
        compiler_params=pltpu.CompilerParams(
            collective_id=1, has_side_effects=True, vmem_limit_bytes=VMEM_LIMIT
        ),
        name="first",
    )(halo_source[0], halo_count, field, masks, weights, targets)

    block = pl.BlockSpec((3, ROWS, LANES), lambda b: (0, b, 0))
    first, second = pl.pallas_call(
        functools.partial(second_kernel, groups, ndev),
        grid=(count // ROWS,),
        out_shape=(shape(planes.shape, F32), shape(planes.shape, F32)),
        in_specs=[vmem()] * 5,
        out_specs=(block, block),
        scratch_shapes=[pltpu.VMEM((4 * halo, 384), BF16)],
        compiler_params=pltpu.CompilerParams(vmem_limit_bytes=VMEM_LIMIT),
        name="second",
    )(first, masks, weights, targets, second_halo)
    return jnp.transpose(first, (1, 0, 2)), jnp.transpose(second, (1, 0, 2))


def solution(mesh):
    whole = P(("group", "dev"))
    return jax.shard_map(
        functools.partial(local, mesh.shape["group"], mesh.shape["dev"]),
        mesh=mesh,
        in_specs=(
            P(("group", "dev"), None, None),
            whole,
            whole,
            whole,
            whole,
            P(("group", "dev"), None, None),
            P(("group", "dev"), None, None),
            P(("group", "dev"), None),
            P(),
            P(),
            P(),
        ),
        out_specs=(P(("group", "dev"), None, None), P(("group", "dev"), None, None)),
        check_vma=False,
    )
```

profile of v0, /device:TPU:24, one launch (start us, length us, event | category | flops | bytes accessed | tf_op | source)
XLA Modules:
  0.0 166.8 jit_solution(10029843339064241049)
XLA Ops:
  0.6 1.3 reshape.27.target_ref
  1.9 4.4 %plan.1 = (s32[32,128]{1,0:T(8,128)}, f32[256,128]{1,0:T(8,128)}) custom-call(s32[16,128]{1,0:T(8,128)} %bitcast.13, s32[16,128]{1,0:T(8,128)} %bitcast.14, s32[16,128]{1,0:T(8,128)} %bitcast.15), custom_call_target="tpu_custom_call" | custom-call | tf_op jit(solution)/shard_map/plan/pallas_call | solution.py:429
  6.3 106.4 %exchange.1 = (f32[7680,128]{1,0:T(8,128)}, s32[16,128]{1,0:T(8,128)}, f32[64,128]{1,0:T(8,128)}, bf16[1920,768]{1,0:T(8,128)(2,1)}) custom-call(s32[32,128]{1,0:T(8,128)} %get-tuple-element.12.source_ref, f32[3,2048,128]{2,1,0:T(8,128)} %bitcast.11, f32[256,128]{1,0:T(8,128)} %get-tuple-element.13.meta_ref, s32[16,128]{1,0:T(8,128)} %bitcast.12, ...), custom_call_target="tpu_custom_call" | custom-call | tf_op jit(solution)/shard_map/exchange/pallas_call | solution.py:438
  112.7 0.0 copy-start
  112.7 7.2 %gather.1.field_ref = f32[3,2064,128]{2,1,0:T(8,128)} custom-call(s32[16,128]{1,0:T(8,128)} %get-tuple-element.14.inverse_ref, f32[7680,128]{1,0:T(8,128)} %get-tuple-element.15.recv_ref), custom_call_target="tpu_custom_call" | custom-call | tf_op jit(solution)/shard_map/gather/pallas_call | solution.py:463
  119.9 0.0 copy-done
  119.9 1.3 copy.13
  121.2 28.1 %first.1 = (f32[3,2064,128]{2,1,0:T(8,128)}, f32[2,192,128]{2,1,0:T(8,128)}) custom-call(s32[2,64]{1,0:T(2,128)} %bitcast.16, s32[1,2]{1,0:T(1,128)} %count_ref.1, f32[3,2064,128]{2,1,0:T(8,128)} %gather.1.field_ref, f32[2048,4]{1,0:T(8,128)} %bitcast.9, bf16[1920,768]{1,0:T(8,128)(2,1)} %get-tuple-element.17.weights_ref, s32[1,128]{1,0:T(1,128)} %reshape.27.target_ref), custom_call_target="tpu_custom_call" | custom-call | tf_op jit(solution)/shard_map/first/pallas_call | solution.py:474
  149.4 17.4 %second.1 = (f32[3,2048,128]{2,1,0:T(8,128)}, f32[3,2048,128]{2,1,0:T(8,128)}) custom-call(f32[3,2064,128]{2,1,0:T(8,128)} %get-tuple-element.18.field_ref, f32[2048,4]{1,0:T(8,128)} %bitcast.10, bf16[1920,768]{1,0:T(8,128)(2,1)} %get-tuple-element.17.weights_ref, s32[1,128]{1,0:T(1,128)} %reshape.27.target_ref, f32[2,192,128]{2,1,0:T(8,128)} %get-tuple-element.19.arrived_ref), custom_call_target="tpu_custom_call" | custom-call | tf_op jit(solution)/shard_map/second/pallas_call | solution.py:494
  (1 shorter events, 0.0 us)
Async XLA Ops:
  112.7 7.2 %copy-start = (f32[64,128]{1,0:T(8,128)S(1)}, f32[64,128]{1,0:T(8,128)}, u32[]{:S(2)}) copy-start(f32[64,128]{1,0:T(8,128)} %get-tuple-element.16) | copy-start | bytes 98308
where the time goes:
time: 167 us
  Pallas kernels  163 us (98%)
  local copies, waits for them, and re-layouts  2.64 us (2%)
    pallas_call x1, Pallas kernels, local(): pl.pallas_call(functools.partial(exchange_kernel, ndev, capacity), out_sh...  106 us
    pallas_call x1, Pallas kernels, local(): pl.pallas_call(functools.partial(first_kernel, groups, ndev), out_shape=(...  28.1 us
    pallas_call x1, Pallas kernels, local(): pl.pallas_call(functools.partial(second_kernel, groups, ndev), grid=(coun...  17.4 us
    pallas_call x1, Pallas kernels, local(): pl.pallas_call(functools.partial(gather_kernel, capacity), out_shape=shap...  7.16 us
    pallas_call x1, Pallas kernels, local(): pl.pallas_call(functools.partial(plan_kernel, ndev), out_shape=(shape((nd...  4.38 us

commit v1 on v0

--- a/solution.py
+++ b/solution.py
@@ -77,31 +77,52 @@
 
 
 def exchange_kernel(
+    groups,
     ndev,
     capacity,
     source_ref,
+    halo_source_ref,
+    count_ref,
     tiles_ref,
     meta_ref,
     flags_ref,
     stiffness_ref,
     nitsche_ref,
     coupling_ref,
-    recv_ref,
-    inverse_ref,
+    target_ref,
+    first_ref,
     masks_ref,
     weights_ref,
+    second_halo_ref,
     send_ref,
+    recv_ref,
     meta_recv_ref,
+    arrival_masks_ref,
+    own_ref,
+    near_ref,
+    sums_ref,
+    inverse_ref,
+    inverse_smem,
+    halo_send_ref,
+    arrived_ref,
+    arrived2_ref,
+    images_ref,
     send_sem,
     recv_sem,
     meta_send_sem,
     meta_recv_sem,
     own_sem,
+    halo_send_sem,
+    halo_recv_sem,
 ):
     me = lax.axis_index("dev")
     x, z = me // NZ, me % NZ
     nx = ndev // NZ
     chunk = 3 * capacity
+    halo = halo_source_ref.shape[1]
+    count = first_ref.shape[1] - 2 * PAD
+    curve, prior, after = neighbours(groups, ndev)
+    has_prev, has_next = curve > 0, curve < groups * ndev - 1
 
     def offset(step):
         return (11 * step) % ndev
@@ -135,6 +156,19 @@
             device_id_type=MESH,
         )
 
+    def halo_copies(turn, into):
+        return [
+            pltpu.make_async_remote_copy(
+                src_ref=halo_send_ref.at[turn, side],
+                dst_ref=into.at[1 - side, pl.ds(0, 3 * halo)],
+                send_sem=halo_send_sem.at[turn, side],
+                recv_sem=halo_recv_sem.at[turn, side],
+                device_id=(prior, after)[side],
+                device_id_type=MESH,
+            )
+            for side in range(2)
+        ]
+
     def pack(off):
         to = peer(off)
         base = pl.multiple_of(off * chunk, 8)
@@ -151,7 +185,9 @@
             barrier, inc=1, device_id={"dev": peer(offset(step))}, device_id_type=MESH
         )
 
-    pl.semaphore_wait(barrier, ndev - 1)
+    for other in (prior, after):
+        pl.semaphore_signal(barrier, inc=1, device_id=other, device_id_type=MESH)
+    pl.semaphore_wait(barrier, ndev + 1)
 
     @pl.loop(1, ndev)
     def _(step):
@@ -190,6 +226,9 @@
     kind = iota((3 * blocks, LANES), 0) // blocks
     high_of = iota((3 * blocks, LANES), 0) % blocks + 1
     rank = iota((1, LANES), 1)
+    flag_bits = flags_ref[...].astype(F32).astype(BF16)
+    diagonal = (iota((LANES, LANES), 0) == iota((LANES, LANES), 1)).astype(F32).astype(BF16)
+    term = iota((8, LANES), 0)
 
     def place(off, total):
         base = pl.multiple_of(off * 8, 8)
@@ -201,38 +240,148 @@
             jnp.where(kind == 1, rank.astype(F32), level),
         )
         value = jnp.where(high == high_of, value, 0.0)
-        column = (low == iota((LANES, LANES), 0)).astype(F32)
-        return total + nt_dot(value.astype(BF16), column.astype(BF16))
+        column = (low == iota((LANES, LANES), 0)).astype(F32).astype(BF16)
+        flag = jnp.where(high == iota((blocks, LANES), 0) + 1, dot(flag_bits, column), 0.0)
+        flag = jnp.sum(flag, axis=0, keepdims=True)
+        bits = jnp.where(term == 3, flag, (level == term.astype(F32)).astype(F32))
+        across = nt_dot(diagonal, bits.astype(BF16))
+        arrival_masks_ref[pl.ds(pl.multiple_of(off * capacity, 8), capacity), :] = across[:capacity]
+        return total + nt_dot(value.astype(BF16), column)
 
     total = lax.fori_loop(0, ndev, place, jnp.zeros((3 * blocks, LANES), F32))
-    inverse_ref[...] = (total[:blocks] * float(chunk) + total[blocks : 2 * blocks]).astype(I32)
+    arrival = (total[:blocks] * float(chunk) + total[blocks : 2 * blocks] * 3.0).astype(I32)
+    inverse_ref[...] = jnp.clip(arrival, 0, (ndev - 1) * chunk + chunk - 3)
+    to_smem = pltpu.make_async_copy(inverse_ref, inverse_smem, own_sem.at[2])
+    to_smem.start()
     level = total[2 * blocks :]
     masks_ref[...] = jnp.concatenate(
         [(level == float(index)).astype(F32) for index in range(3)] + [flags_ref[...].astype(F32)],
         axis=0,
     )
 
+    def products(pair):
+        offs = [offset(2 * pair + i) for i in range(2)]
+        bases = [pl.multiple_of(off * chunk, 8) for off in offs]
+        columns = jnp.concatenate(
+            [
+                arrival_masks_ref[pl.ds(pl.multiple_of(off * capacity, 8), capacity), :]
+                for off in offs
+            ],
+            axis=0,
+        )
+        masks = [columns[:, l : l + 1].astype(BF16) for l in range(4)]
+        high, low = [], []
+        for p in range(3):
+            h, l = halves(
+                jnp.concatenate(
+                    [recv_ref[pl.ds(base + p * capacity, capacity), :] for base in bases], axis=0
+                )
+            )
+            high.append(h)
+            low.append(l)
+        result = dot(jnp.concatenate([h * m for m in masks for h in high], axis=1), weights_ref[0:1536, :])
+        own = (
+            result[:, :384]
+            + result[:, 384:]
+            + dot(jnp.concatenate([l * m for m in masks for l in low], axis=1), weights_ref[0:1536, 0:384])
+        )
+        result = dot(jnp.concatenate(high, axis=1), weights_ref[1536:1920, :])
+        near = (
+            result[:, :384]
+            + result[:, 384:]
+            + dot(jnp.concatenate(low, axis=1), weights_ref[1536:1920, 0:384])
+        )
+        for i, base in enumerate(bases):
+            part = slice(i * capacity, (i + 1) * capacity)
+            for p in range(3):
+                rows = pl.ds(base + p, capacity, stride=3)
+                own_ref[rows, :] = own[part, p * LANES : (p + 1) * LANES]
+                near_ref[rows, :] = near[part, p * LANES : (p + 1) * LANES]
+
     own_rows.wait()
-
-    @pl.loop(1, ndev)
-    def _(step):
-        data_copy(step).wait()
-
-
-def gather_kernel(capacity, inverse_ref, recv_ref, field_ref):
-    blocks = inverse_ref.shape[0]
-    count = blocks * LANES
+    data_copy(1).wait()
+    products(0)
+
+    @pl.loop(1, ndev // 2)
+    def _(pair):
+        data_copy(2 * pair).wait()
+        data_copy(2 * pair + 1).wait()
+        products(pair)
+
+    def arrival_of(block, lane):
+        return jnp.clip(inverse_smem[block, lane], 0, (ndev - 1) * chunk + chunk - 3)
+
+    to_smem.wait()
+    for side in range(2):
+        for k in range(halo):
+            slot = halo_source_ref[side, k]
+            row = arrival_of(slot // LANES, slot % LANES)
+            halo_send_ref[0, side, pl.ds(3 * k, 3), :] = near_ref[pl.ds(row, 3), :]
+        live = iota((3 * halo, LANES), 0) < 3 * count_ref[0, side]
+        halo_send_ref[0, side] = jnp.where(live, halo_send_ref[0, side], 0.0)
+
+    def gather(block, carry):
+        before, here, row = carry
+        base = pl.multiple_of(block * (3 * LANES), 8)
+        for k in range(LANES):
+            if k < LANES - 1:
+                later = arrival_of(block, k + 1)
+                ahead = near_ref[pl.ds(later, 3), :]
+            else:
+                later = arrival_of(jnp.minimum(block + 1, blocks - 1), 0)
+                ahead = jnp.where(block < blocks - 1, near_ref[pl.ds(later, 3), :], 0.0)
+            sums_ref[pl.ds(base + 3 * k, 3), :] = own_ref[pl.ds(row, 3), :] + (before + ahead)
+            before, here, row = here, ahead, later
+        return before, here, row
+
+    row = arrival_of(0, 0)
+    start = (jnp.zeros((3, LANES), F32), near_ref[pl.ds(row, 3), :], row)
+    start = gather(0, start)
+    sent = halo_copies(0, arrived_ref)
+    for copy in sent:
+        copy.start()
+    lax.fori_loop(1, blocks, gather, start)
     for p in range(3):
-        field_ref[p, 0:PAD, :] = jnp.zeros((PAD, LANES), F32)
-        field_ref[p, PAD + count : 2 * PAD + count, :] = jnp.zeros((PAD, LANES), F32)
-
-    @pl.loop(0, blocks)
+        first_ref[p, 0:PAD, :] = jnp.zeros((PAD, LANES), F32)
+        first_ref[p, PAD + count : 2 * PAD + count, :] = jnp.zeros((PAD, LANES), F32)
+
+    for copy in sent:
+        copy.wait()
+    rows = []
+    for side, alive in ((0, has_prev), (1, has_next)):
+        row = jnp.concatenate(
+            [arrived_ref[side, pl.ds(p, halo, stride=3), :] for p in range(3)], axis=1
+        )
+        rows.append(jnp.where(alive, row, 0.0))
+    high, low = halves(jnp.concatenate(rows, axis=0))
+    images_ref[0 : 2 * halo, :] = high
+    images_ref[2 * halo : 4 * halo, :] = low
+
+    @pl.loop(0, count // ROWS)
     def _(block):
-        base = pl.multiple_of(block * LANES, 8)
-        for k in range(LANES):
-            row = inverse_ref[block, k]
+        added = halo_block(target_ref, images_ref, block)
+        base = pl.multiple_of(block * (3 * ROWS), 8)
+        rows = pl.ds(pl.multiple_of(block * ROWS, ROWS) + PAD, ROWS)
+        for p in range(3):
+            first_ref[p, rows, :] = (
+                sums_ref[pl.ds(base + p, ROWS, stride=3), :] + added[:, p * LANES : (p + 1) * LANES]
+            )
+
+    for side in range(2):
+        for k in range(halo):
+            row = halo_source_ref[side, k] + PAD
             for p in range(3):
-                field_ref[p, pl.ds(base + (PAD + k), 1), :] = recv_ref[pl.ds(row + p * capacity, 1), :]
+                halo_send_ref[1, side, pl.ds(p * halo + k, 1), :] = first_ref[p, pl.ds(row, 1), :]
+        live = iota((halo, LANES), 0) < count_ref[0, side]
+        for p in range(3):
+            part = pl.ds(p * halo, halo)
+            halo_send_ref[1, side, part, :] = jnp.where(live, halo_send_ref[1, side, part, :], 0.0)
+    sent = halo_copies(1, arrived2_ref)
+    for copy in sent:
+        copy.start()
+    for copy in sent:
+        copy.wait()
+    second_halo_ref[...] = arrived2_ref[:, 0 : 3 * halo, :]
 
 
 def operator_block(field_ref, masks_ref, weights_ref, block):
@@ -282,97 +431,6 @@
     total = groups * ndev
     after, prior = (me + 1) % total, (me + total - 1) % total
     return me, (prior // ndev, prior % ndev), (after // ndev, after % ndev)
-
-
-def first_kernel(
-    groups,
-    ndev,
-    source_ref,
-    count_ref,
-    field_ref,
-    masks_ref,
-    weights_ref,
-    target_ref,
-    first_ref,
-    second_halo_ref,
-    send_ref,
-    arrived_ref,
-    arrived2_ref,
-    images_ref,
-    send_sem,
-    recv_sem,
-):
-    halo = source_ref.shape[1]
-    blocks = (field_ref.shape[1] - 2 * PAD) // ROWS
-    me, prior, after = neighbours(groups, ndev)
-    has_prev, has_next = me > 0, me < groups * ndev - 1
-
-    barrier = pltpu.get_barrier_semaphore()
-    for other in (prior, after):
-        pl.semaphore_signal(barrier, inc=1, device_id=other, device_id_type=MESH)
-    pl.semaphore_wait(barrier, 2)
-
-    def copies(turn, into):
-        return [
-            pltpu.make_async_remote_copy(
-                src_ref=send_ref.at[turn, side],
-                dst_ref=into.at[1 - side],
-                send_sem=send_sem.at[turn, side],
-                recv_sem=recv_sem.at[turn, side],
-                device_id=(prior, after)[side],
-                device_id_type=MESH,
-            )
-            for side in range(2)
-        ]
-
-    def pack(turn, rows_ref):
-        for side in range(2):
-            for k in range(halo):
-                row = source_ref[side, k] + PAD
-                for p in range(3):
-                    send_ref[turn, side, pl.ds(p * halo + k, 1), :] = rows_ref[p, pl.ds(row, 1), :]
-            live = iota((halo, LANES), 0) < count_ref[0, side]
-            for p in range(3):
-                part = pl.ds(p * halo, halo)
-                send_ref[turn, side, part, :] = jnp.where(live, send_ref[turn, side, part, :], 0.0)
-
-    def local(block):
-        result = operator_block(field_ref, masks_ref, weights_ref, block)
-        rows = pl.ds(pl.multiple_of(block * ROWS, ROWS) + PAD, ROWS)
-        for p in range(3):
-            first_ref[p, rows, :] = result[:, p * LANES : (p + 1) * LANES]
-
-    pack(0, field_ref)
-    for p in range(3):
-        first_ref[p, 0:PAD, :] = jnp.zeros((PAD, LANES), F32)
-        first_ref[p, PAD + blocks * ROWS : 2 * PAD + blocks * ROWS, :] = jnp.zeros((PAD, LANES), F32)
-    local(0)
-    sent = copies(0, arrived_ref)
-    for copy in sent:
-        copy.start()
-
-    @pl.loop(1, blocks)
-    def _(block):
-        local(block)
-
-    for copy in sent:
-        copy.wait()
-    halo_images(arrived_ref, weights_ref, images_ref, has_prev, has_next, halo)
-
-    @pl.loop(0, blocks)
-    def _(block):
-        added = halo_block(target_ref, images_ref, block)
-        rows = pl.ds(pl.multiple_of(block * ROWS, ROWS) + PAD, ROWS)
-        for p in range(3):
-            first_ref[p, rows, :] = first_ref[p, rows, :] + added[:, p * LANES : (p + 1) * LANES]
-
-    pack(1, first_ref)
-    sent = copies(1, arrived2_ref)
-    for copy in sent:
-        copy.start()
-    for copy in sent:
-        copy.wait()
-    second_halo_ref[...] = arrived2_ref[...]
 
 
 def second_kernel(
@@ -435,61 +493,57 @@
     )(new_owner.reshape(by_lane), new_slot.reshape(by_lane), levels.reshape(by_lane))
 
     arrivals = ndev * 3 * capacity
-    recv, inverse, masks, weights = pl.pallas_call(
-        functools.partial(exchange_kernel, ndev, capacity),
+    targets = halo_target.reshape(1, 2 * halo)
+    first, masks, weights, second_halo = pl.pallas_call(
+        functools.partial(exchange_kernel, groups, ndev, capacity),
         out_shape=(
-            shape((arrivals, LANES), F32),
-            shape(by_lane, I32),
+            shape((3, count + 2 * PAD, LANES), F32),
             shape((4 * blocks, LANES), F32),
             shape((1920, 768), BF16),
+            shape((2, 3 * halo, LANES), F32),
         ),
-        in_specs=[smem()] + [vmem()] * 6,
-        out_specs=(hbm(), vmem(), vmem(), vmem()),
+        in_specs=[smem()] * 3 + [vmem()] * 7,
+        out_specs=(vmem(), vmem(), vmem(), vmem()),
         scratch_shapes=[
             pltpu.VMEM((arrivals, LANES), F32),
+            pltpu.VMEM((arrivals, LANES), F32),
             pltpu.VMEM((8 * ndev, LANES), F32),
+            pltpu.VMEM((ndev * capacity, 8), F32),
+            pltpu.VMEM((arrivals + 8, LANES), F32),
+            pltpu.VMEM((arrivals + 8, LANES), F32),
+            pltpu.VMEM((3 * count + 8, LANES), F32),
+            pltpu.VMEM(by_lane, I32),
+            pltpu.SMEM(by_lane, I32),
+            pltpu.VMEM((2, 2, 3 * halo, LANES), F32),
+            pltpu.VMEM((2, 3 * halo + 8, LANES), F32),
+            pltpu.VMEM((2, 3 * halo + 8, LANES), F32),
+            pltpu.VMEM((4 * halo, 384), BF16),
             pltpu.SemaphoreType.DMA((ndev,)),
             pltpu.SemaphoreType.DMA((ndev,)),
             pltpu.SemaphoreType.DMA((ndev,)),
             pltpu.SemaphoreType.DMA((ndev,)),
-            pltpu.SemaphoreType.DMA((2,)),
+            pltpu.SemaphoreType.DMA((3,)),
+            pltpu.SemaphoreType.DMA((2, 2)),
+            pltpu.SemaphoreType.DMA((2, 2)),
         ],
         compiler_params=pltpu.CompilerParams(
             collective_id=0, has_side_effects=True, vmem_limit_bytes=VMEM_LIMIT
         ),
         name="exchange",
-    )(source, planes, meta, flags.reshape(by_lane), stiffness, nitsche, coupling)
-
-    field = pl.pallas_call(
-        functools.partial(gather_kernel, capacity),
-        out_shape=shape((3, count + 2 * PAD, LANES), F32),
-        in_specs=[smem(), vmem()],
-        out_specs=vmem(),
-        compiler_params=pltpu.CompilerParams(vmem_limit_bytes=VMEM_LIMIT),
-        name="gather",
-    )(inverse, recv)
+    )(
+        source,
+        halo_source[0],
+        halo_count,
+        planes,
+        meta,
+        flags.reshape(by_lane),
+        stiffness,
+        nitsche,
+        coupling,
+        targets,
+    )
 
     masks = masks.reshape(4, count).T
-    targets = halo_target.reshape(1, 2 * halo)
-    first, second_halo = pl.pallas_call(
-        functools.partial(first_kernel, groups, ndev),
-        out_shape=(shape(field.shape, F32), shape((2, 3 * halo, LANES), F32)),
-        in_specs=[smem(), smem()] + [vmem()] * 4,
-        out_specs=(vmem(), vmem()),
-        scratch_shapes=[
-            pltpu.VMEM((2, 2, 3 * halo, LANES), F32),
-            pltpu.VMEM((2, 3 * halo, LANES), F32),
-            pltpu.VMEM((2, 3 * halo, LANES), F32),
-            pltpu.VMEM((4 * halo, 384), BF16),
-            pltpu.SemaphoreType.DMA((2, 2)),
-            pltpu.SemaphoreType.DMA((2, 2)),
-        ],
-        compiler_params=pltpu.CompilerParams(
-            collective_id=1, has_side_effects=True, vmem_limit_bytes=VMEM_LIMIT
-        ),
-        name="first",
-    )(halo_source[0], halo_count, field, masks, weights, targets)
-
     block = pl.BlockSpec((3, ROWS, LANES), lambda b: (0, b, 0))
     first, second = pl.pallas_call(
         functools.partial(second_kernel, groups, ndev),

time: 167 us -> 149 us (0.89)
  Pallas kernels: 163 us -> 145 us
    pallas_call x3 -> x1, Pallas kernels: 142 us -> 123 us  [local(): pl.pallas_call(functools.partial(exchange_kernel, groups, ndev, capacity)...]
where the time goes in v1:
time: 149 us
  Pallas kernels  145 us (97%)
  local copies, waits for them, and re-layouts  3.42 us (2%)
    pallas_call x1, Pallas kernels, local(): pl.pallas_call(functools.partial(exchange_kernel, groups, ndev, capacity)...  123 us
    pallas_call x1, Pallas kernels, local(): pl.pallas_call(functools.partial(second_kernel, groups, ndev), grid=(coun...  17.4 us
    pallas_call x1, Pallas kernels, local(): pl.pallas_call(functools.partial(plan_kernel, ndev), out_shape=(shape((nd...  4.38 us

profile of v1, /device:TPU:24, one launch (start us, length us, event | category | flops | bytes accessed | tf_op | source)
XLA Modules:
  0.0 148.9 jit_solution(16850325985219871365)
XLA Ops:
  0.6 1.3 reshape.26.target_ref
  1.9 4.4 %plan.1 = (s32[32,128]{1,0:T(8,128)}, f32[256,128]{1,0:T(8,128)}) custom-call(s32[16,128]{1,0:T(8,128)} %bitcast.12, s32[16,128]{1,0:T(8,128)} %bitcast.13, s32[16,128]{1,0:T(8,128)} %bitcast.14), custom_call_target="tpu_custom_call" | custom-call | tf_op jit(solution)/shard_map/plan/pallas_call | solution.py:487
  6.3 123.1 %exchange.1 = (f32[3,2064,128]{2,1,0:T(8,128)}, f32[64,128]{1,0:T(8,128)}, bf16[1920,768]{1,0:T(8,128)(2,1)}, f32[2,192,128]{2,1,0:T(8,128)}) custom-call(s32[32,128]{1,0:T(8,128)} %get-tuple-element.10.source_ref, s32[2,64]{1,0:T(2,128)} %bitcast.15, s32[1,2]{1,0:T(1,128)} %count_ref.1, f32[3,2048,128]{2,1,0:T(8,128)} %bitcast.10, ...), custom_call_target="tpu_custom_call" | custom-call | tf_op jit(solution)/shard_map/exchange/pallas_call | solution.py:497
  129.4 0.8 reshape.27
  130.2 1.3 copy.13
  131.5 17.4 %second.1 = (f32[3,2048,128]{2,1,0:T(8,128)}, f32[3,2048,128]{2,1,0:T(8,128)}) custom-call(f32[3,2064,128]{2,1,0:T(8,128)} %get-tuple-element.12.field_ref, f32[2048,4]{1,0:T(8,128)} %bitcast.9, bf16[1920,768]{1,0:T(8,128)(2,1)} %get-tuple-element.14.weights_ref, s32[1,128]{1,0:T(1,128)} %reshape.26.target_ref, f32[2,192,128]{2,1,0:T(8,128)} %get-tuple-element.15.arrived_ref), custom_call_target="tpu_custom_call" | custom-call | tf_op jit(solution)/shard_map/second/pallas_call | solution.py:548

commit v2 on v1

--- a/solution.py
+++ b/solution.py
@@ -386,7 +386,21 @@
 
 def operator_block(field_ref, masks_ref, weights_ref, block):
     base = pl.multiple_of(block * ROWS, ROWS)
-    columns = masks_ref[pl.ds(pl.multiple_of(block * ROWS, ROWS), ROWS), :]
+    diagonal = (iota((LANES, LANES), 0) == iota((LANES, LANES), 1)).astype(F32).astype(BF16)
+    lanes = masks_ref.shape[0] // 4
+    columns = jnp.concatenate(
+        [
+            nt_dot(
+                diagonal,
+                jnp.concatenate(
+                    [masks_ref[pl.ds(l * lanes + block * (ROWS // LANES) + j, 1), :] for l in range(4)],
+                    axis=0,
+                ).astype(BF16),
+            )
+            for j in range(ROWS // LANES)
+        ],
+        axis=0,
+    )
     masks = [columns[:, l : l + 1].astype(BF16) for l in range(4)]
     high, low, beside_high, beside_low = [], [], [], []
     for p in range(3):
@@ -543,7 +557,6 @@
         targets,
     )
 
-    masks = masks.reshape(4, count).T
     block = pl.BlockSpec((3, ROWS, LANES), lambda b: (0, b, 0))
     first, second = pl.pallas_call(
         functools.partial(second_kernel, groups, ndev),

time: 149 us -> 148 us (level)
  local copies, waits for them, and re-layouts: 3.42 us -> 1.29 us
    reshape x2 -> x0, local copies, waits for them, and re-layouts: 2.12 us -> none  [local(): masks = masks.reshape(4, count).T]
where the time goes in v2:
time: 148 us
  Pallas kernels  146 us (99%)
    pallas_call x1, Pallas kernels, local(): pl.pallas_call(functools.partial(exchange_kernel, groups, ndev, capacity)...  123 us
    pallas_call x1, Pallas kernels, local(): pl.pallas_call(functools.partial(second_kernel, groups, ndev), grid=(coun...  18.3 us
    pallas_call x1, Pallas kernels, local(): pl.pallas_call(functools.partial(plan_kernel, ndev), out_shape=(shape((nd...  4.38 us

profile of v2, /device:TPU:24, one launch (start us, length us, event | category | flops | bytes accessed | tf_op | source)
XLA Modules:
  0.0 147.7 jit_solution(16072656079068227765)
XLA Ops:
  0.6 1.3 reshape.23.target_ref
  1.9 4.4 %plan.1 = (s32[32,128]{1,0:T(8,128)}, f32[256,128]{1,0:T(8,128)}) custom-call(s32[16,128]{1,0:T(8,128)} %bitcast.10, s32[16,128]{1,0:T(8,128)} %bitcast.11, s32[16,128]{1,0:T(8,128)} %bitcast.12), custom_call_target="tpu_custom_call" | custom-call | tf_op jit(solution)/shard_map/plan/pallas_call | solution.py:501
  6.3 123.1 %exchange.1 = (f32[3,2064,128]{2,1,0:T(8,128)}, f32[64,128]{1,0:T(8,128)}, bf16[1920,768]{1,0:T(8,128)(2,1)}, f32[2,192,128]{2,1,0:T(8,128)}) custom-call(s32[32,128]{1,0:T(8,128)} %get-tuple-element.10.source_ref, s32[2,64]{1,0:T(2,128)} %bitcast.13, s32[1,2]{1,0:T(1,128)} %count_ref.1, f32[3,2048,128]{2,1,0:T(8,128)} %bitcast.8, ...), custom_call_target="tpu_custom_call" | custom-call | tf_op jit(solution)/shard_map/exchange/pallas_call | solution.py:511
  129.4 18.3 %second.1 = (f32[3,2048,128]{2,1,0:T(8,128)}, f32[3,2048,128]{2,1,0:T(8,128)}) custom-call(f32[3,2064,128]{2,1,0:T(8,128)} %get-tuple-element.12.field_ref, f32[64,128]{1,0:T(8,128)} %get-tuple-element.13.masks_ref, bf16[1920,768]{1,0:T(8,128)(2,1)} %get-tuple-element.14.weights_ref, s32[1,128]{1,0:T(1,128)} %reshape.23.target_ref, ...), custom_call_target="tpu_custom_call" | custom-call | tf_op jit(solution)/shard_map/second/pallas_call | solution.py:561
